TPU v7x, 256 devices: a whole 4x4x8 slice. The times are simulated.
256 devices in a mesh: dp: 16 (over z_hi, y, core), seq: 16 (over x, z_lo).
Axes of the slice: x: 4, y: 4, z: 8 (z_hi: 2, z_lo: 4; z = z_hi * 4 + z_lo), core: 2. Of those that a mesh axis runs over, the one named last changes fastest.
Arguments:
- inputs: bfloat16 [2, 65536, 2048], P(None, 'seq', 'dp'), may hold values from -6 to 6
- cotangent: bfloat16 [2, 65536, 2048], P(None, 'seq', 'dp'), may hold values from -6 to 6
- kernel: bfloat16 [65536, 2048], P('seq', 'dp'), may hold values from -6 to 6
- factor_one: bfloat16 [256, 256], replicated, may hold values from -0.375 to 0.375
- factor_two: bfloat16 [256, 256], replicated, may hold values from -0.375 to 0.375
Outputs:
- grad_inputs: bfloat16 [2, 65536, 2048], P(None, 'seq', 'dp')
- grad_kernel: bfloat16 [65536, 2048], P('seq', 'dp')
- grad_factor_one: float32 [256, 256], replicated
- grad_factor_two: float32 [256, 256], replicated
All inputs are finite; a program needn't handle non-finite values.
Results may differ from a plain program's by a relative error of at most 0.0085.
Values may be sent and summed in bfloat16 or wider, within the bound.
A program may use at most 128 MiB of HBM per device.

v0:
```python
import math
import jax
import jax.numpy as jnp
from jax import lax
from jax.sharding import PartitionSpec as P


def within_blocks(factor, values):
    return jnp.einsum("cb,nabh->nach", factor, values, preferred_element_type=jnp.float32)


def within_blocks_back(factor, values):
    return jnp.einsum("cb,nach->nabh", factor, values, preferred_element_type=jnp.float32)


def across_blocks(factor, values):
    return jnp.einsum("ea,nach->nech", factor, values, preferred_element_type=jnp.float32)


def across_blocks_back(factor, values):
    return jnp.einsum("ea,nech->nach", factor, values, preferred_element_type=jnp.float32)


def pair_product(left, right):
    return jnp.einsum("nech,nach->ea", left, right, preferred_element_type=jnp.float32)


def on_device(inputs, cotangent, kernel, factor_one, factor_two):
    batch_count = inputs.shape[0]
    row_count = inputs.shape[1]
    channels = inputs.shape[2]
    block_size = factor_one.shape[0]
    block_count = factor_two.shape[0]
    local_blocks = row_count // block_size
    inputs_cube = inputs.reshape(batch_count, local_blocks, block_size, channels)
    grads_cube = cotangent.reshape(batch_count, local_blocks, block_size, channels)
    kernel_cube = kernel.reshape(local_blocks, block_size, channels)
    within_mix = within_blocks(factor_one, inputs_cube).astype(jnp.bfloat16)
    within_spread = lax.all_to_all(within_mix, "seq", split_axis=2, concat_axis=1, tiled=True)
    spectrum = across_blocks(factor_two, within_spread).astype(jnp.bfloat16)
    grad_within = within_blocks(factor_one, grads_cube).astype(jnp.bfloat16)
    grad_spread = lax.all_to_all(grad_within, "seq", split_axis=2, concat_axis=1, tiled=True)
    grad_spectrum = across_blocks(factor_two, grad_spread).astype(jnp.bfloat16)
    spectrum_home, grad_spectrum_home = (
        lax.all_to_all(spectrum, "seq", split_axis=1, concat_axis=2, tiled=True),
        lax.all_to_all(grad_spectrum, "seq", split_axis=1, concat_axis=2, tiled=True),
    )
    kernel_wide = kernel_cube.astype(jnp.float32)[None]
    weighted_home = (kernel_wide * spectrum_home.astype(jnp.float32)).astype(jnp.bfloat16)
    grad_weighted_home = (kernel_wide * grad_spectrum_home.astype(jnp.float32)).astype(jnp.bfloat16)
    kernel_terms = jnp.sum(
        grad_spectrum_home.astype(jnp.float32) * spectrum_home.astype(jnp.float32), axis=0
    )
    weighted, grad_weighted = (
        lax.all_to_all(weighted_home, "seq", split_axis=2, concat_axis=1, tiled=True),
        lax.all_to_all(grad_weighted_home, "seq", split_axis=2, concat_axis=1, tiled=True),
    )
    returned_spread = across_blocks_back(factor_two, weighted).astype(jnp.bfloat16)
    grad_returned_spread = across_blocks_back(factor_two, grad_weighted).astype(jnp.bfloat16)
    second_terms = pair_product(weighted, grad_spread) + pair_product(grad_weighted, within_spread)
    returned, grad_returned = (
        lax.all_to_all(returned_spread, "seq", split_axis=1, concat_axis=2, tiled=True),
        lax.all_to_all(grad_returned_spread, "seq", split_axis=1, concat_axis=2, tiled=True),
    )
    grad_inputs = within_blocks_back(factor_one, grad_returned).astype(jnp.bfloat16)
    first_terms = jnp.einsum(
        "nach,nabh->cb", returned, grads_cube, preferred_element_type=jnp.float32
    )
    first_terms = first_terms + jnp.einsum(
        "nach,nabh->cb", grad_returned, inputs_cube, preferred_element_type=jnp.float32
    )
    first_total, second_total = lax.psum((first_terms, second_terms), ("dp", "seq"))
    kernel_half = kernel_terms.astype(jnp.bfloat16)
    grad_kernel = kernel_half.reshape(row_count, channels)
    full_width = channels * lax.axis_size("dp")
    scale_first = 1.0 / math.sqrt(batch_count * block_count * full_width)
    scale_second = 1.0 / math.sqrt(batch_count * block_size * full_width)
    return (
        grad_inputs.reshape(batch_count, row_count, channels),
        grad_kernel,
        first_total * scale_first,
        second_total * scale_second,
    )


def solution(mesh):
    return jax.shard_map(
        on_device,
        mesh=mesh,
        in_specs=(P(None, "seq", "dp"), P(None, "seq", "dp"), P("seq", "dp"), P(), P()),
        out_specs=(P(None, "seq", "dp"), P("seq", "dp"), P(), P()),
        check_vma=False,
    )
```

profile of v0, /device:TPU:2, one launch (start us, length us, event | category | flops | bytes accessed | tf_op | source)
XLA Modules:
  0.0 732.7 jit_solution(2225070951256302418)
XLA Ops:
  7.2 3.8 convert_bitcast_fusion.2
  11.0 4.6 copy.99
  15.6 9.0 %all-to-all-start.4 = ((bf16[2,16,256,128]{3,1,0,2:T(8,128)(2,1)}), bf16[2,16,256,128]{3,1,0,2:T(8,128)(2,1)}, u32[]{:S(2)}, u32[]{:S(2)}) async-start(bf16[2,16,256,128]{3,1,0,2:T(8,128)(2,1)} %copy.99), calls=%async_computation.4 | async-start | bytes 4194304 | tf_op jit(solution)/shard_map/all_to_all | solution.py:39
  24.6 2.1 convert_bitcast_fusion.6
  26.7 4.6 copy.82
  31.3 41.4 %all-to-all-done.4 = bf16[2,16,256,128]{3,1,0,2:T(8,128)(2,1)} async-done(((bf16[2,16,256,128]{3,1,0,2:T(8,128)(2,1)}), bf16[2,16,256,128]{3,1,0,2:T(8,128)(2,1)}, u32[]{:S(2)}, u32[]{:S(2)}) %all-to-all-start.4) | async-done | bytes 2097184 | tf_op jit(solution)/shard_map/all_to_all | solution.py:39
  72.6 6.7 all-to-all-start
  79.3 2.4 copy.101
  83.1 2.5 convert_bitcast_fusion.1
  85.6 4.5 copy.103
  90.1 36.7 %all-to-all-done = bf16[2,16,256,128]{3,1,0,2:T(8,128)(2,1)} async-done(((bf16[2,16,256,128]{3,1,0,2:T(8,128)(2,1)}), bf16[2,16,256,128]{3,1,0,2:T(8,128)(2,1)}, u32[]{:S(2)}, u32[]{:S(2)}) %all-to-all-start) | async-done | bytes 2097184 | tf_op jit(solution)/shard_map/all_to_all | solution.py:42
  126.8 6.8 all-to-all-start.5
  133.6 2.4 copy.84
  137.4 2.4 convert_bitcast_fusion.5
  139.9 4.5 copy.86
  144.4 36.7 %all-to-all-done.5 = bf16[2,256,16,128]{3,2,0,1:T(8,128)(2,1)} async-done(((bf16[2,256,16,128]{3,2,0,1:T(8,128)(2,1)}), bf16[2,256,16,128]{3,2,0,1:T(8,128)(2,1)}, u32[]{:S(2)}, u32[]{:S(2)}) %all-to-all-start.5) | async-done | bytes 2097184 | tf_op jit(solution)/shard_map/all_to_all | solution.py:45
  181.1 6.9 all-to-all-start.1
  188.0 2.8 convert.11
  190.7 1.9 copy_convert_fusion
  192.6 2.5 copy.108
  195.1 40.3 %all-to-all-done.1 = bf16[2,256,16,128]{3,2,0,1:T(8,128)(2,1)} async-done(((bf16[2,256,16,128]{3,2,0,1:T(8,128)(2,1)}), bf16[2,256,16,128]{3,2,0,1:T(8,128)(2,1)}, u32[]{:S(2)}, u32[]{:S(2)}) %all-to-all-start.1) | async-done | bytes 2097184 | tf_op jit(solution)/shard_map/all_to_all | solution.py:46
  235.5 1.9 copy_convert_fusion.1
  240.2 2.4 fusion
  242.6 2.7 copy.109
  245.3 6.8 all-to-all-start.6
  252.1 4.3 copy.89
  256.4 43.2 %all-to-all-done.6 = bf16[2,16,256,128]{3,1,0,2:T(8,128)(2,1)} async-done(((bf16[2,16,256,128]{3,1,0,2:T(8,128)(2,1)}), bf16[2,16,256,128]{3,1,0,2:T(8,128)(2,1)}, u32[]{:S(2)}, u32[]{:S(2)}) %all-to-all-start.6) | async-done | bytes 2097184 | tf_op jit(solution)/shard_map/all_to_all | solution.py:55
  299.6 6.8 all-to-all-start.2
  306.4 2.4 copy.111
  310.1 2.4 convert_bitcast_fusion
  312.6 4.6 copy.113
  317.1 36.8 %all-to-all-done.2 = bf16[2,16,256,128]{3,1,0,2:T(8,128)(2,1)} async-done(((bf16[2,16,256,128]{3,1,0,2:T(8,128)(2,1)}), bf16[2,16,256,128]{3,1,0,2:T(8,128)(2,1)}, u32[]{:S(2)}, u32[]{:S(2)}) %all-to-all-start.2) | async-done | bytes 2097184 | tf_op jit(solution)/shard_map/all_to_all | solution.py:56
  353.9 6.8 all-to-all-start.7
  360.8 2.4 copy.91
  364.5 2.4 convert_bitcast_fusion.4
  367.0 4.5 copy.93
  371.5 36.8 %all-to-all-done.7 = bf16[2,256,16,128]{3,2,0,1:T(8,128)(2,1)} async-done(((bf16[2,256,16,128]{3,2,0,1:T(8,128)(2,1)}), bf16[2,256,16,128]{3,2,0,1:T(8,128)(2,1)}, u32[]{:S(2)}, u32[]{:S(2)}) %all-to-all-start.7) | async-done | bytes 2097184 | tf_op jit(solution)/shard_map/all_to_all | solution.py:62
  408.3 6.8 all-to-all-start.3
  415.4 2.8 multiply_reduce_fusion
  419.7 1.9 copy.106
  423.6 3.0 fusion.37
  426.6 1.9 fusion.47
  428.6 2.2 copy.115
  431.5 31.1 %all-to-all-done.3 = bf16[2,256,16,128]{3,2,0,1:T(8,128)(2,1)} async-done(((bf16[2,256,16,128]{3,2,0,1:T(8,128)(2,1)}), bf16[2,256,16,128]{3,2,0,1:T(8,128)(2,1)}, u32[]{:S(2)}, u32[]{:S(2)}) %all-to-all-start.3) | async-done | bytes 2097184 | tf_op jit(solution)/shard_map/all_to_all | solution.py:63
  462.6 2.3 copy.95
  467.7 3.7 convert_bitcast_fusion.3
  471.4 3.9 copy.97
  475.4 248.7 %all-reduce.3.cloned.1.call-done = (f32[256,256]{1,0:T(8,128)}, f32[256,256]{1,0:T(8,128)}) async-done(((f32[256,256]{1,0:T(8,128)}, f32[256,256]{1,0:T(8,128)}), (f32[256,256]{1,0:T(8,128)}, f32[256,256]{1,0:T(8,128)})) %all-reduce.3.cloned.1.call-update) | async-done | bytes 524304 | tf_op jit(solution)/shard_map/psum | solution.py:72
  (36 shorter events, 17.4 us)
Async XLA Ops:
  7.2 17.4 %copy-start = (bf16[2,4096,128]{2,1,0:T(8,128)(2,1)S(1)}, bf16[2,4096,128]{2,1,0:T(8,128)(2,1)}, u32[]{:S(2)}) copy-start(bf16[2,4096,128]{2,1,0:T(8,128)(2,1)} %param.6) | copy-start | bytes 6291460
  15.6 9.0 %copy-start.13 = (bf16[256,256]{1,0:T(8,128)(2,1)S(1)}, bf16[256,256]{1,0:T(8,128)(2,1)}, u32[]{:S(2)}) copy-start(bf16[256,256]{1,0:T(8,128)(2,1)} %param.8) | copy-start | bytes 393220
  15.6 57.0 %all-to-all-start.4 = ((bf16[2,16,256,128]{3,1,0,2:T(8,128)(2,1)}), bf16[2,16,256,128]{3,1,0,2:T(8,128)(2,1)}, u32[]{:S(2)}, u32[]{:S(2)}) async-start(bf16[2,16,256,128]{3,1,0,2:T(8,128)(2,1)} %copy.99), calls=%async_computation.4 | async-start | bytes 4194304 | tf_op jit(solution)/shard_map/all_to_all | solution.py:39
  72.6 54.2 %all-to-all-start = ((bf16[2,16,256,128]{3,1,0,2:T(8,128)(2,1)}), bf16[2,16,256,128]{3,1,0,2:T(8,128)(2,1)}, u32[]{:S(2)}, u32[]{:S(2)}) async-start(bf16[2,16,256,128]{3,1,0,2:T(8,128)(2,1)} %copy.82), calls=%async_computation | async-start | bytes 4194304 | tf_op jit(solution)/shard_map/all_to_all | solution.py:42
  79.3 3.8 copy-start.11
  81.7 1.4 copy-start.3
  126.8 54.3 %all-to-all-start.5 = ((bf16[2,256,16,128]{3,2,0,1:T(8,128)(2,1)}), bf16[2,256,16,128]{3,2,0,1:T(8,128)(2,1)}, u32[]{:S(2)}, u32[]{:S(2)}) async-start(bf16[2,256,16,128]{3,2,0,1:T(8,128)(2,1)} %copy.103), calls=%async_computation.5 | async-start | bytes 4194304 | tf_op jit(solution)/shard_map/all_to_all | solution.py:45
  136.0 1.4 copy-start.5
  181.1 54.4 %all-to-all-start.1 = ((bf16[2,256,16,128]{3,2,0,1:T(8,128)(2,1)}), bf16[2,256,16,128]{3,2,0,1:T(8,128)(2,1)}, u32[]{:S(2)}, u32[]{:S(2)}) async-start(bf16[2,256,16,128]{3,2,0,1:T(8,128)(2,1)} %copy.86), calls=%async_computation.1 | async-start | bytes 4194304 | tf_op jit(solution)/shard_map/all_to_all | solution.py:46
  237.4 2.2 copy-start.1
  237.4 2.9 copy-start.2
  245.3 54.3 %all-to-all-start.6 = ((bf16[2,16,256,128]{3,1,0,2:T(8,128)(2,1)}), bf16[2,16,256,128]{3,1,0,2:T(8,128)(2,1)}, u32[]{:S(2)}, u32[]{:S(2)}) async-start(bf16[2,16,256,128]{3,1,0,2:T(8,128)(2,1)} %copy.109), calls=%async_computation.6 | async-start | bytes 4194304 | tf_op jit(solution)/shard_map/all_to_all | solution.py:55
  299.6 54.3 %all-to-all-start.2 = ((bf16[2,16,256,128]{3,1,0,2:T(8,128)(2,1)}), bf16[2,16,256,128]{3,1,0,2:T(8,128)(2,1)}, u32[]{:S(2)}, u32[]{:S(2)}) async-start(bf16[2,16,256,128]{3,1,0,2:T(8,128)(2,1)} %copy.89), calls=%async_computation.2 | async-start | bytes 4194304 | tf_op jit(solution)/shard_map/all_to_all | solution.py:56
  308.8 1.3 copy-start.7
  353.9 54.3 %all-to-all-start.7 = ((bf16[2,256,16,128]{3,2,0,1:T(8,128)(2,1)}), bf16[2,256,16,128]{3,2,0,1:T(8,128)(2,1)}, u32[]{:S(2)}, u32[]{:S(2)}) async-start(bf16[2,256,16,128]{3,2,0,1:T(8,128)(2,1)} %copy.113), calls=%async_computation.7 | async-start | bytes 4194304 | tf_op jit(solution)/shard_map/all_to_all | solution.py:62
  363.2 1.3 copy-start.8
  408.3 54.3 %all-to-all-start.3 = ((bf16[2,256,16,128]{3,2,0,1:T(8,128)(2,1)}), bf16[2,256,16,128]{3,2,0,1:T(8,128)(2,1)}, u32[]{:S(2)}, u32[]{:S(2)}) async-start(bf16[2,256,16,128]{3,2,0,1:T(8,128)(2,1)} %copy.93), calls=%async_computation.3 | async-start | bytes 4194304 | tf_op jit(solution)/shard_map/all_to_all | solution.py:63
  415.1 308.9 %all-reduce.3.cloned.1.call-start = ((), (), s32[]{:S(2)}) async-start(), calls=%async_computation.8 | async-start | bytes 1048576 | tf_op jit(solution)/shard_map/psum | solution.py:72
  421.7 2.0 copy-start.6
  423.6 3.0 copy-start.4
  423.6 3.0 copy-start.9
  462.6 3.7 copy-start.12
  464.9 1.3 copy-start.10
Sparse Core Ops, SparseCore 0:
  467.8 256.1 all-reduce.2
where the time goes:
time: 734 us; the launch traced here: 733 us
  waiting for transfers between devices  552 us (75%)
  local copies, waits for them, and re-layouts  69.9 us (10%)
  starting transfers between devices  57 us (8%)
  matrix products  26.5 us (4%)
  between operations  14.2 us (2%)
  other arithmetic  13.5 us (2%)
    psum x1, waiting for transfers between devices, on_device(): lax.psum((first_terms, second_terms), ('dp', 'seq'))  249 us
    all_to_all x1, waiting for transfers between devices, on_device(): lax.all_to_all(weighted_home, 'seq', split_axis=2, concat_axis=1, tiled=T...  43.2 us
    all_to_all x1, waiting for transfers between devices, on_device(): lax.all_to_all(within_mix, 'seq', split_axis=2, concat_axis=1, tiled=True)  41.4 us
    all_to_all x1, waiting for transfers between devices, on_device(): lax.all_to_all(grad_spectrum, 'seq', split_axis=1, concat_axis=2, tiled=T...  40.3 us
    all_to_all x1, waiting for transfers between devices, on_device(): lax.all_to_all(grad_weighted_home, 'seq', split_axis=2, concat_axis=1, ti...  36.8 us
    all_to_all x1, waiting for transfers between devices, on_device(): lax.all_to_all(returned_spread, 'seq', split_axis=1, concat_axis=2, tiled...  36.8 us
    all_to_all x1, waiting for transfers between devices, on_device(): lax.all_to_all(spectrum, 'seq', split_axis=1, concat_axis=2, tiled=True)  36.7 us
    all_to_all x1, waiting for transfers between devices, on_device(): lax.all_to_all(grad_within, 'seq', split_axis=2, concat_axis=1, tiled=True)  36.7 us
  transfers between devices with their start and end apart: 9, of which 9 were waited for; matrix products, arithmetic and copies ran while one was open for 11% of the time, Pallas kernels for 0%

commit v1 on v0

--- a/solution.py
+++ b/solution.py
@@ -36,7 +36,10 @@
     grads_cube = cotangent.reshape(batch_count, local_blocks, block_size, channels)
     kernel_cube = kernel.reshape(local_blocks, block_size, channels)
     within_mix = within_blocks(factor_one, inputs_cube).astype(jnp.bfloat16)
-    within_spread = lax.all_to_all(within_mix, "seq", split_axis=2, concat_axis=1, tiled=True)
+    within_spread = jnp.concatenate(
+        lax.all_to_all(jnp.stack(jnp.split(within_mix, lax.axis_size("seq"), axis=2)), "seq", 0, 0),
+        axis=1,
+    )
     spectrum = across_blocks(factor_two, within_spread).astype(jnp.bfloat16)
     grad_within = within_blocks(factor_one, grads_cube).astype(jnp.bfloat16)
     grad_spread = lax.all_to_all(grad_within, "seq", split_axis=2, concat_axis=1, tiled=True)

time: 734 us -> 786 us (1.071)
  local copies, waits for them, and re-layouts: 69.9 us -> 122 us
    another operation x1 -> x19, local copies, waits for them, and re-layouts: 1.92 us -> 41.4 us  [the longest x18 39.5 us: on_device(): jnp.stack(jnp.split(within_mix, lax.axis_size('seq'), axis=2))]
    unnamed x29 -> x52, local copies, waits for them, and re-layouts: 11.3 us -> 28.6 us
  transfers between devices with their start and end apart: 9 -> 9, of which waited for: 9 -> 9; matrix products, arithmetic and copies ran while one was open for 11% -> 10% of each run, Pallas kernels for 0% -> 0%
where the time goes in v1:
time: 786 us; the launch traced here: 784 us
  waiting for transfers between devices  552 us (70%)
  local copies, waits for them, and re-layouts  122 us (16%)
  starting transfers between devices  56.8 us (7%)
  matrix products  25.2 us (3%)
  between operations  14.3 us (2%)
  other arithmetic  13.5 us (2%)
    psum x1, waiting for transfers between devices, on_device(): lax.psum((first_terms, second_terms), ('dp', 'seq'))  249 us
    all_to_all x1, waiting for transfers between devices, on_device(): lax.all_to_all(weighted_home, 'seq', split_axis=2, concat_axis=1, tiled=T...  43.2 us
    all_to_all x1, waiting for transfers between devices, on_device(): lax.all_to_all(jnp.stack(jnp.split(within_mix, lax.axis_size('seq'), axis...  41.3 us
    all_to_all x1, waiting for transfers between devices, on_device(): lax.all_to_all(grad_spectrum, 'seq', split_axis=1, concat_axis=2, tiled=T...  40.3 us
    another operation x18, local copies, waits for them, and re-layouts, on_device(): jnp.stack(jnp.split(within_mix, lax.axis_size('seq'), axis=2))  39.5 us
    all_to_all x1, waiting for transfers between devices, on_device(): lax.all_to_all(grad_within, 'seq', split_axis=2, concat_axis=1, tiled=True)  37.1 us
    all_to_all x1, waiting for transfers between devices, on_device(): lax.all_to_all(returned_spread, 'seq', split_axis=1, concat_axis=2, tiled...  36.8 us
    all_to_all x1, waiting for transfers between devices, on_device(): lax.all_to_all(grad_weighted_home, 'seq', split_axis=2, concat_axis=1, ti...  36.8 us
  transfers between devices with their start and end apart: 9, of which 9 were waited for; matrix products, arithmetic and copies ran while one was open for 10% of the time, Pallas kernels for 0%

profile of v1, /device:TPU:2, one launch (start us, length us, event | category | flops | bytes accessed | tf_op | source)
XLA Modules:
  0.0 783.6 jit_solution(11918454290747151906)
XLA Ops:
  7.2 2.5 convert_bitcast_fusion.2
  9.7 7.6 slice_bitcast_fusion
  19.5 2.2 copy.97
  21.7 2.2 copy.98
  26.1 2.2 copy.100
  30.4 2.2 copy.102
  32.6 2.2 copy.103
  39.2 2.2 copy.106
  43.5 2.2 copy.108
  66.5 9.0 %all-to-all-start.4 = ((bf16[16,2,16,16,128]{4,3,2,1,0:T(8,128)(2,1)}), bf16[16,2,16,16,128]{4,3,2,1,0:T(8,128)(2,1)}, u32[]{:S(2)}, u32[]{:S(2)}) async-start(bf16[16,2,16,16,128]{4,3,2,1,0:T(8,128)(2,1)} %constant_dynamic-update-slice_fusion), calls=%async_computation.4 | async-start | bytes 4194304 | tf_op jit(solution)/shard_map/all_to_all | solution.py:40
  77.6 4.5 copy.79
  82.2 41.3 %all-to-all-done.4 = bf16[16,2,16,16,128]{4,3,2,1,0:T(8,128)(2,1)} async-done(((bf16[16,2,16,16,128]{4,3,2,1,0:T(8,128)(2,1)}), bf16[16,2,16,16,128]{4,3,2,1,0:T(8,128)(2,1)}, u32[]{:S(2)}, u32[]{:S(2)}) %all-to-all-start.4) | async-done | bytes 2097184 | tf_op jit(solution)/shard_map/all_to_all | solution.py:40
  123.5 6.7 all-to-all-start
  133.6 2.5 convert_bitcast_fusion.1
  136.0 4.6 copy.114
  140.6 37.1 %all-to-all-done = bf16[2,16,256,128]{3,1,0,2:T(8,128)(2,1)} async-done(((bf16[2,16,256,128]{3,1,0,2:T(8,128)(2,1)}), bf16[2,16,256,128]{3,1,0,2:T(8,128)(2,1)}, u32[]{:S(2)}, u32[]{:S(2)}) %all-to-all-start) | async-done | bytes 2097184 | tf_op jit(solution)/shard_map/all_to_all | solution.py:45
  177.7 6.8 all-to-all-start.5
  184.5 2.4 copy.81
  188.3 2.5 convert_bitcast_fusion.5
  190.8 4.5 copy.83
  195.3 36.7 %all-to-all-done.5 = bf16[2,256,16,128]{3,2,0,1:T(8,128)(2,1)} async-done(((bf16[2,256,16,128]{3,2,0,1:T(8,128)(2,1)}), bf16[2,256,16,128]{3,2,0,1:T(8,128)(2,1)}, u32[]{:S(2)}, u32[]{:S(2)}) %all-to-all-start.5) | async-done | bytes 2097184 | tf_op jit(solution)/shard_map/all_to_all | solution.py:48
  232.0 6.8 all-to-all-start.1
  238.9 2.8 convert.11
  243.5 2.5 copy.119
  246.0 40.3 %all-to-all-done.1 = bf16[2,256,16,128]{3,2,0,1:T(8,128)(2,1)} async-done(((bf16[2,256,16,128]{3,2,0,1:T(8,128)(2,1)}), bf16[2,256,16,128]{3,2,0,1:T(8,128)(2,1)}, u32[]{:S(2)}, u32[]{:S(2)}) %all-to-all-start.1) | async-done | bytes 2097184 | tf_op jit(solution)/shard_map/all_to_all | solution.py:49
  291.1 2.4 fusion
  293.5 2.7 copy.120
  296.2 6.9 all-to-all-start.6
  303.0 4.3 copy.86
  307.3 43.2 %all-to-all-done.6 = bf16[2,16,256,128]{3,1,0,2:T(8,128)(2,1)} async-done(((bf16[2,16,256,128]{3,1,0,2:T(8,128)(2,1)}), bf16[2,16,256,128]{3,1,0,2:T(8,128)(2,1)}, u32[]{:S(2)}, u32[]{:S(2)}) %all-to-all-start.6) | async-done | bytes 2097184 | tf_op jit(solution)/shard_map/all_to_all | solution.py:58
  350.5 6.8 all-to-all-start.2
  357.3 2.4 copy.122
  361.1 2.4 convert_bitcast_fusion
  363.5 4.6 copy.124
  368.1 36.8 %all-to-all-done.2 = bf16[2,16,256,128]{3,1,0,2:T(8,128)(2,1)} async-done(((bf16[2,16,256,128]{3,1,0,2:T(8,128)(2,1)}), bf16[2,16,256,128]{3,1,0,2:T(8,128)(2,1)}, u32[]{:S(2)}, u32[]{:S(2)}) %all-to-all-start.2) | async-done | bytes 2097184 | tf_op jit(solution)/shard_map/all_to_all | solution.py:59
  404.8 6.8 all-to-all-start.7
  411.7 2.4 copy.88
  415.4 2.4 convert_bitcast_fusion.4
  417.9 4.5 copy.90
  422.4 36.8 %all-to-all-done.7 = bf16[2,256,16,128]{3,2,0,1:T(8,128)(2,1)} async-done(((bf16[2,256,16,128]{3,2,0,1:T(8,128)(2,1)}), bf16[2,256,16,128]{3,2,0,1:T(8,128)(2,1)}, u32[]{:S(2)}, u32[]{:S(2)}) %all-to-all-start.7) | async-done | bytes 2097184 | tf_op jit(solution)/shard_map/all_to_all | solution.py:65
  459.2 6.8 all-to-all-start.3
  466.1 2.8 multiply_reduce_fusion
  474.3 3.0 fusion.37
  482.2 31.3 %all-to-all-done.3 = bf16[2,256,16,128]{3,2,0,1:T(8,128)(2,1)} async-done(((bf16[2,256,16,128]{3,2,0,1:T(8,128)(2,1)}), bf16[2,256,16,128]{3,2,0,1:T(8,128)(2,1)}, u32[]{:S(2)}, u32[]{:S(2)}) %all-to-all-start.3) | async-done | bytes 2097184 | tf_op jit(solution)/shard_map/all_to_all | solution.py:66
  513.5 2.3 copy.92
  518.6 3.7 convert_bitcast_fusion.3
  522.3 3.9 copy.94
  526.3 248.7 %all-reduce.3.cloned.1.call-done = (f32[256,256]{1,0:T(8,128)}, f32[256,256]{1,0:T(8,128)}) async-done(((f32[256,256]{1,0:T(8,128)}, f32[256,256]{1,0:T(8,128)}), (f32[256,256]{1,0:T(8,128)}, f32[256,256]{1,0:T(8,128)})) %all-reduce.3.cloned.1.call-update) | async-done | bytes 524304 | tf_op jit(solution)/shard_map/psum | solution.py:75
  (76 shorter events, 64.9 us)
Async XLA Ops:
  7.2 68.3 %copy-start = (bf16[2,4096,128]{2,1,0:T(8,128)(2,1)S(1)}, bf16[2,4096,128]{2,1,0:T(8,128)(2,1)}, u32[]{:S(2)}) copy-start(bf16[2,4096,128]{2,1,0:T(8,128)(2,1)} %param.6) | copy-start | bytes 6291460
  49.2 12.6 %copy-start.17 = (bf16[1,2,16,16,128]{4,3,2,1,0:T(8,128)(2,1)S(1)}, bf16[1,2,16,16,128]{4,3,2,1,0:T(8,128)(2,1)}, u32[]{:S(2)}) copy-start(bf16[1,2,16,16,128]{4,3,2,1,0:T(8,128)(2,1)} %copy.105) | copy-start | bytes 393220
  49.2 13.3 %copy-start.16 = (bf16[1,2,16,16,128]{4,3,2,1,0:T(8,128)(2,1)S(1)}, bf16[1,2,16,16,128]{4,3,2,1,0:T(8,128)(2,1)}, u32[]{:S(2)}) copy-start(bf16[1,2,16,16,128]{4,3,2,1,0:T(8,128)(2,1)} %copy.106) | copy-start | bytes 393220
  49.2 14.0 %copy-start.15 = (bf16[1,2,16,16,128]{4,3,2,1,0:T(8,128)(2,1)S(1)}, bf16[1,2,16,16,128]{4,3,2,1,0:T(8,128)(2,1)}, u32[]{:S(2)}) copy-start(bf16[1,2,16,16,128]{4,3,2,1,0:T(8,128)(2,1)} %copy.107) | copy-start | bytes 393220
  49.2 14.6 %copy-start.14 = (bf16[1,2,16,16,128]{4,3,2,1,0:T(8,128)(2,1)S(1)}, bf16[1,2,16,16,128]{4,3,2,1,0:T(8,128)(2,1)}, u32[]{:S(2)}) copy-start(bf16[1,2,16,16,128]{4,3,2,1,0:T(8,128)(2,1)} %copy.108) | copy-start | bytes 393220
  66.5 9.0 %copy-start.13 = (bf16[256,256]{1,0:T(8,128)(2,1)S(1)}, bf16[256,256]{1,0:T(8,128)(2,1)}, u32[]{:S(2)}) copy-start(bf16[256,256]{1,0:T(8,128)(2,1)} %param.8) | copy-start | bytes 393220
  66.5 57.0 %all-to-all-start.4 = ((bf16[16,2,16,16,128]{4,3,2,1,0:T(8,128)(2,1)}), bf16[16,2,16,16,128]{4,3,2,1,0:T(8,128)(2,1)}, u32[]{:S(2)}, u32[]{:S(2)}) async-start(bf16[16,2,16,16,128]{4,3,2,1,0:T(8,128)(2,1)} %constant_dynamic-update-slice_fusion), calls=%async_computation.4 | async-start | bytes 4194304 | tf_op jit(solution)/shard_map/all_to_all | solution.py:40
  123.5 54.2 %all-to-all-start = ((bf16[2,16,256,128]{3,1,0,2:T(8,128)(2,1)}), bf16[2,16,256,128]{3,1,0,2:T(8,128)(2,1)}, u32[]{:S(2)}, u32[]{:S(2)}) async-start(bf16[2,16,256,128]{3,1,0,2:T(8,128)(2,1)} %copy.79), calls=%async_computation | async-start | bytes 4194304 | tf_op jit(solution)/shard_map/all_to_all | solution.py:45
  130.2 3.4 copy-start.11
  132.2 1.4 copy-start.3
  177.7 54.3 %all-to-all-start.5 = ((bf16[2,256,16,128]{3,2,0,1:T(8,128)(2,1)}), bf16[2,256,16,128]{3,2,0,1:T(8,128)(2,1)}, u32[]{:S(2)}, u32[]{:S(2)}) async-start(bf16[2,256,16,128]{3,2,0,1:T(8,128)(2,1)} %copy.114), calls=%async_computation.5 | async-start | bytes 4194304 | tf_op jit(solution)/shard_map/all_to_all | solution.py:48
  186.9 1.4 copy-start.5
  232.0 54.3 %all-to-all-start.1 = ((bf16[2,256,16,128]{3,2,0,1:T(8,128)(2,1)}), bf16[2,256,16,128]{3,2,0,1:T(8,128)(2,1)}, u32[]{:S(2)}, u32[]{:S(2)}) async-start(bf16[2,256,16,128]{3,2,0,1:T(8,128)(2,1)} %copy.83), calls=%async_computation.1 | async-start | bytes 4194304 | tf_op jit(solution)/shard_map/all_to_all | solution.py:49
  288.2 2.2 copy-start.1
  288.3 2.9 copy-start.2
  296.2 54.3 %all-to-all-start.6 = ((bf16[2,16,256,128]{3,1,0,2:T(8,128)(2,1)}), bf16[2,16,256,128]{3,1,0,2:T(8,128)(2,1)}, u32[]{:S(2)}, u32[]{:S(2)}) async-start(bf16[2,16,256,128]{3,1,0,2:T(8,128)(2,1)} %copy.120), calls=%async_computation.6 | async-start | bytes 4194304 | tf_op jit(solution)/shard_map/all_to_all | solution.py:58
  350.5 54.3 %all-to-all-start.2 = ((bf16[2,16,256,128]{3,1,0,2:T(8,128)(2,1)}), bf16[2,16,256,128]{3,1,0,2:T(8,128)(2,1)}, u32[]{:S(2)}, u32[]{:S(2)}) async-start(bf16[2,16,256,128]{3,1,0,2:T(8,128)(2,1)} %copy.86), calls=%async_computation.2 | async-start | bytes 4194304 | tf_op jit(solution)/shard_map/all_to_all | solution.py:59
  359.8 1.3 copy-start.7
  404.8 54.3 %all-to-all-start.7 = ((bf16[2,256,16,128]{3,2,0,1:T(8,128)(2,1)}), bf16[2,256,16,128]{3,2,0,1:T(8,128)(2,1)}, u32[]{:S(2)}, u32[]{:S(2)}) async-start(bf16[2,256,16,128]{3,2,0,1:T(8,128)(2,1)} %copy.124), calls=%async_computation.7 | async-start | bytes 4194304 | tf_op jit(solution)/shard_map/all_to_all | solution.py:65
  414.1 1.3 copy-start.8
  459.2 54.3 %all-to-all-start.3 = ((bf16[2,256,16,128]{3,2,0,1:T(8,128)(2,1)}), bf16[2,256,16,128]{3,2,0,1:T(8,128)(2,1)}, u32[]{:S(2)}, u32[]{:S(2)}) async-start(bf16[2,256,16,128]{3,2,0,1:T(8,128)(2,1)} %copy.90), calls=%async_computation.3 | async-start | bytes 4194304 | tf_op jit(solution)/shard_map/all_to_all | solution.py:66
  466.0 308.9 %all-reduce.3.cloned.1.call-start = ((), (), s32[]{:S(2)}) async-start(), calls=%async_computation.8 | async-start | bytes 1048576 | tf_op jit(solution)/shard_map/psum | solution.py:75
  472.4 2.0 copy-start.6
  474.3 3.0 copy-start.4
  474.3 3.0 copy-start.9
  513.5 3.7 copy-start.12
  515.9 1.3 copy-start.10
Sparse Core Ops, SparseCore 0:
  518.8 256.1 all-reduce.2
